TPU v7x, 32 devices: a whole 2x2x4 slice. The times are simulated.
32 devices in a mesh: dp: 8 (over y, x, core), fsdp: 4 (over z).
Axes of the slice: x: 2, y: 2, z: 4, core: 2. Of those that a mesh axis runs over, the one named last changes fastest.
Arguments:
- tokens: bfloat16 [46400, 1024], P(('dp', 'fsdp')), may hold values from -6 to 6
- output_grad: bfloat16 [46400, 1024], P(('dp', 'fsdp')), may hold values from -6 to 6
- group_member: int32 [8], P('dp'), may hold values from 0 to 1, as said below
- image_counts: int32 [2], replicated, may hold values from 64 to 4095
- position_source: int32 [145, 4], replicated, may hold values from 0 to 49
- position_table: bfloat16 [50, 1024], P(None, 'fsdp'), may hold values from -3 to 3
- first_gain: bfloat16 [1024], P('fsdp'), may hold values from 0.5 to 1.5
- first_shift: bfloat16 [1024], P('fsdp'), may hold values from -1 to 1
- input_proj: bfloat16 [1024, 3072], P('fsdp'), may hold values from -0.1875 to 0.1875
- query_bias: bfloat16 [1024], P('fsdp'), may hold values from -1 to 1
- value_bias: bfloat16 [1024], P('fsdp'), may hold values from -1 to 1
- output_proj: bfloat16 [1024, 1024], P('fsdp'), may hold values from -0.75 to 0.75
- output_bias: bfloat16 [1024], P('fsdp'), may hold values from -1 to 1
- second_gain: bfloat16 [1024], P('fsdp'), may hold values from 0.5 to 1.5
- second_shift: bfloat16 [1024], P('fsdp'), may hold values from -1 to 1
- hidden_weight: bfloat16 [1024, 4096], P('fsdp'), may hold values from -0.1875 to 0.1875
- hidden_bias: bfloat16 [4096], P('fsdp'), may hold values from -1 to 1
- return_weight: bfloat16 [4096, 1024], P('fsdp'), may hold values from -0.09375 to 0.09375
- return_bias: bfloat16 [1024], P('fsdp'), may hold values from -1 to 1
Outputs:
- block_out: bfloat16 [46400, 1024], P(('dp', 'fsdp'))
- tokens_grad: bfloat16 [46400, 1024], P(('dp', 'fsdp'))
- table_grad: float32 [50, 1024], P(None, 'fsdp')
- first_gain_grad: float32 [1024], P('fsdp')
- first_shift_grad: float32 [1024], P('fsdp')
- input_proj_grad: float32 [1024, 3072], P('fsdp')
- query_bias_grad: float32 [1024], P('fsdp')
- value_bias_grad: float32 [1024], P('fsdp')
- output_proj_grad: float32 [1024, 1024], P('fsdp')
- output_bias_grad: float32 [1024], P('fsdp')
- second_gain_grad: float32 [1024], P('fsdp')
- second_shift_grad: float32 [1024], P('fsdp')
- hidden_weight_grad: float32 [1024, 4096], P('fsdp')
- hidden_bias_grad: float32 [4096], P('fsdp')
- return_weight_grad: float32 [4096, 1024], P('fsdp')
- return_bias_grad: float32 [1024], P('fsdp')
Inputs may be any that keep to these rules, and one draw needn't show every extreme that they name: `group_member`: exactly 3 entries are 1, the others 0.
All inputs are finite; a program needn't handle non-finite values.
Results may differ from a plain program's by a relative error of at most 0.02.
Values may be sent and summed in bfloat16 or wider, within the bound.
No kernel may reach another device: no remote copies, remote signals or barrier semaphores. Data moves between devices by JAX's collectives and lax.ppermute only.
A program may use at most 320 MiB of HBM per device.

v0:
```python
from functools import partial
import math
import jax
import jax.numpy as jnp
from jax import lax
from jax.sharding import PartitionSpec as P

D = 1024
HEADS = 16
HEAD_DIM = 64
SG = 7
LG = 12
SMALL_LEN = 50
LARGE_LEN = 145
ROWS = 1450
EPS = 1e-06


def shortened(value):
    return jax.tree.map(lambda a: a.astype(jnp.bfloat16) if a.dtype == jnp.float32 else a, value)


def grid_fraction(index):
    scaled = jnp.maximum((2 * index + 1) * SG - LG, 0)
    lower = scaled // (2 * LG)
    return (scaled - 2 * LG * lower).astype(jnp.float32) / (2.0 * LG)


def interp_table(position_source):
    position = jnp.arange(LARGE_LEN, dtype=jnp.int32)
    patch = jnp.maximum(position - 1, 0)
    frac_row = grid_fraction(patch // LG)
    frac_col = grid_fraction(patch % LG)
    weights = jnp.stack(
        [
            (1.0 - frac_row) * (1.0 - frac_col),
            (1.0 - frac_row) * frac_col,
            frac_row * (1.0 - frac_col),
            frac_row * frac_col,
        ],
        axis=1,
    )
    class_row = (jnp.arange(4, dtype=jnp.int32) == 0).astype(jnp.float32)
    weights = jnp.where((position == 0)[:, None], class_row[None, :], weights)
    onehot = (
        position_source[:, :, None] == jnp.arange(SMALL_LEN, dtype=jnp.int32)[None, None, :]
    ).astype(jnp.float32)
    return jnp.sum(weights[:, :, None] * onehot, axis=1)


def layer_norm(values, gain, shift):
    average = jnp.mean(values, axis=-1, keepdims=True)
    centred = values - average
    variance = jnp.mean(centred * centred, axis=-1, keepdims=True)
    inv_std = lax.rsqrt(variance + EPS)
    normed = centred * inv_std
    return (normed * gain + shift, normed, inv_std)


def norm_back(grad_norm, normed, inv_std, gain):
    scaled = grad_norm * gain
    inner = (
        scaled
        - jnp.mean(scaled, axis=-1, keepdims=True)
        - normed * jnp.mean(scaled * normed, axis=-1, keepdims=True)
    )
    return (inv_std * inner, jnp.sum(grad_norm * normed, axis=0), jnp.sum(grad_norm, axis=0))


def image_scores(query_low, keys_low, length):
    images = ROWS // length
    query_img = query_low.reshape(images, length, HEADS, HEAD_DIM)
    keys_img = keys_low.reshape(images, length, HEADS, HEAD_DIM)
    logits = jnp.einsum("nqhd,nkhd->nhqk", query_img, keys_img, preferred_element_type=jnp.float32)
    return (logits / math.sqrt(HEAD_DIM), query_img, keys_img)


def attend_forward(query_low, keys_low, values_low, length):
    images = ROWS // length
    scores, _, _ = image_scores(query_low, keys_low, length)
    highest = jnp.max(scores, axis=-1, keepdims=True)
    log_total = highest + jnp.log(jnp.sum(jnp.exp(scores - highest), axis=-1, keepdims=True))
    probs = jnp.exp(scores - log_total)
    values_img = values_low.reshape(images, length, HEADS, HEAD_DIM)
    attended = jnp.einsum(
        "nhqk,nkhd->nqhd",
        probs.astype(jnp.bfloat16),
        values_img,
        preferred_element_type=jnp.float32,
    )
    lse_rows = jnp.transpose(log_total[..., 0], (0, 2, 1)).reshape(ROWS, HEADS)
    return (attended.reshape(ROWS, D).astype(jnp.bfloat16), lse_rows)


def attend_backward(query_low, keys_low, values_low, lse_rows, grad_att_low, length):
    images = ROWS // length
    scores, query_img, keys_img = image_scores(query_low, keys_low, length)
    log_total = jnp.transpose(lse_rows.reshape(images, length, HEADS), (0, 2, 1))[..., None]
    probs = jnp.exp(scores - log_total)
    values_img = values_low.reshape(images, length, HEADS, HEAD_DIM)
    grad_img = grad_att_low.reshape(images, length, HEADS, HEAD_DIM)
    grad_values = jnp.einsum(
        "nhqk,nqhd->nkhd", probs.astype(jnp.bfloat16), grad_img, preferred_element_type=jnp.float32
    )
    grad_probs = jnp.einsum(
        "nqhd,nkhd->nhqk", grad_img, values_img, preferred_element_type=jnp.float32
    )
    grad_scores = probs * (grad_probs - jnp.sum(grad_probs * probs, axis=-1, keepdims=True))
    grad_scores_low = grad_scores.astype(jnp.bfloat16)
    grad_query = jnp.einsum(
        "nhqk,nkhd->nqhd", grad_scores_low, keys_img, preferred_element_type=jnp.float32
    ) / math.sqrt(HEAD_DIM)
    grad_keys = jnp.einsum(
        "nhqk,nqhd->nkhd", grad_scores_low, query_img, preferred_element_type=jnp.float32
    ) / math.sqrt(HEAD_DIM)
    return (
        grad_query.reshape(ROWS, D).astype(jnp.bfloat16),
        grad_keys.reshape(ROWS, D).astype(jnp.bfloat16),
        grad_values.reshape(ROWS, D).astype(jnp.bfloat16),
    )


def per_device(
    tokens,
    output_grad,
    group_member,
    image_counts,
    position_source,
    position_table,
    first_gain,
    first_shift,
    input_proj,
    query_bias,
    value_bias,
    output_proj,
    output_bias,
    second_gain,
    second_shift,
    hidden_weight,
    hidden_bias,
    return_weight,
    return_bias,
):
    gathered = (
        lax.all_gather(input_proj, "fsdp", axis=0, tiled=True),
        lax.all_gather(output_proj, "fsdp", axis=0, tiled=True),
        lax.all_gather(hidden_weight, "fsdp", axis=0, tiled=True),
        lax.all_gather(return_weight, "fsdp", axis=0, tiled=True),
        lax.all_gather(first_gain, "fsdp", axis=0, tiled=True),
        lax.all_gather(first_shift, "fsdp", axis=0, tiled=True),
        lax.all_gather(query_bias, "fsdp", axis=0, tiled=True),
        lax.all_gather(value_bias, "fsdp", axis=0, tiled=True),
        lax.all_gather(output_bias, "fsdp", axis=0, tiled=True),
        lax.all_gather(second_gain, "fsdp", axis=0, tiled=True),
        lax.all_gather(second_shift, "fsdp", axis=0, tiled=True),
        lax.all_gather(hidden_bias, "fsdp", axis=0, tiled=True),
        lax.all_gather(return_bias, "fsdp", axis=0, tiled=True),
        lax.all_gather(position_table, "fsdp", axis=1, tiled=True),
    )
    (
        joint_proj,
        outproj_full,
        hidden_full,
        return_full,
        gain_one,
        shift_one,
        query_add,
        value_add,
        output_add,
        gain_two,
        shift_two,
        hidden_add,
        return_add,
        table_full,
    ) = gathered
    member = group_member[0]
    is_large = member == 1
    length = jnp.where(is_large, LARGE_LEN, SMALL_LEN)
    row_index = jnp.arange(ROWS, dtype=jnp.int32)
    place = row_index % length
    inter = interp_table(position_source)
    identity = (
        jnp.arange(LARGE_LEN, dtype=jnp.int32)[:, None]
        == jnp.arange(SMALL_LEN, dtype=jnp.int32)[None, :]
    ).astype(jnp.float32)
    mixing = jnp.where(is_large, inter, identity)
    picker = (place[:, None] == jnp.arange(LARGE_LEN, dtype=jnp.int32)[None, :]).astype(jnp.float32)
    spread = jnp.dot(picker, mixing, precision=lax.Precision.HIGHEST)
    position = jnp.dot(spread, table_full.astype(jnp.float32), precision=lax.Precision.HIGHEST)
    stream = tokens.astype(jnp.float32) + position
    first_out, first_hat, first_inv = layer_norm(
        stream, gain_one.astype(jnp.float32), shift_one.astype(jnp.float32)
    )
    first_low = first_out.astype(jnp.bfloat16)
    projected = jnp.dot(first_low, joint_proj, preferred_element_type=jnp.float32)
    query_low = (projected[:, :D] + query_add.astype(jnp.float32)).astype(jnp.bfloat16)
    keys_low = projected[:, D : 2 * D].astype(jnp.bfloat16)
    values_low = (projected[:, 2 * D :] + value_add.astype(jnp.float32)).astype(jnp.bfloat16)
    attended_low, lse_rows = lax.cond(
        is_large,
        partial(attend_forward, length=LARGE_LEN),
        partial(attend_forward, length=SMALL_LEN),
        query_low,
        keys_low,
        values_low,
    )
    mid = (
        stream
        + jnp.dot(attended_low, outproj_full, preferred_element_type=jnp.float32)
        + output_add.astype(jnp.float32)
    )
    second_out, second_hat, second_inv = layer_norm(
        mid, gain_two.astype(jnp.float32), shift_two.astype(jnp.float32)
    )
    second_low = second_out.astype(jnp.bfloat16)
    hidden_pre = jnp.dot(
        second_low, hidden_full, preferred_element_type=jnp.float32
    ) + hidden_add.astype(jnp.float32)
    activ, gelu_back = jax.vjp(partial(jax.nn.gelu, approximate=False), hidden_pre)
    activ_low = activ.astype(jnp.bfloat16)
    returned = jnp.dot(
        activ_low, return_full, preferred_element_type=jnp.float32
    ) + return_add.astype(jnp.float32)
    block_out = (mid + returned).astype(jnp.bfloat16)
    again = (
        lax.all_gather(input_proj, "fsdp", axis=0, tiled=True),
        lax.all_gather(output_proj, "fsdp", axis=0, tiled=True),
        lax.all_gather(hidden_weight, "fsdp", axis=0, tiled=True),
        lax.all_gather(return_weight, "fsdp", axis=0, tiled=True),
        lax.all_gather(first_gain, "fsdp", axis=0, tiled=True),
        lax.all_gather(second_gain, "fsdp", axis=0, tiled=True),
    )
    joint_back, outproj_back, hidden_back, return_back, gain_one_back, gain_two_back = again
    grad_out = output_grad.astype(jnp.float32)
    grad_return_w = jnp.einsum(
        "rf,rd->fd", activ_low, output_grad, preferred_element_type=jnp.float32
    )
    grad_return_add = jnp.sum(grad_out, axis=0)
    grad_activ = jnp.einsum(
        "rd,fd->rf", output_grad, return_back, preferred_element_type=jnp.float32
    )
    grad_hidden_low = gelu_back(grad_activ)[0].astype(jnp.bfloat16)
    grad_hidden_w = jnp.einsum(
        "rd,rf->df", second_low, grad_hidden_low, preferred_element_type=jnp.float32
    )
    grad_hidden_add = jnp.sum(grad_hidden_low.astype(jnp.float32), axis=0)
    grad_second = jnp.einsum(
        "rf,df->rd", grad_hidden_low, hidden_back, preferred_element_type=jnp.float32
    )
    grad_mid_norm, grad_gain_two, grad_shift_two = norm_back(
        grad_second, second_hat, second_inv, gain_two_back.astype(jnp.float32)
    )
    grad_mid = grad_out + grad_mid_norm
    grad_branch_low = grad_mid.astype(jnp.bfloat16)
    grad_outproj = jnp.einsum(
        "rd,re->de", attended_low, grad_branch_low, preferred_element_type=jnp.float32
    )
    grad_output_add = jnp.sum(grad_branch_low.astype(jnp.float32), axis=0)
    grad_attended = jnp.einsum(
        "re,de->rd", grad_branch_low, outproj_back, preferred_element_type=jnp.float32
    )
    grad_att_low = grad_attended.astype(jnp.bfloat16)
    grad_query_low, grad_keys_low, grad_values_low = lax.cond(
        is_large,
        partial(attend_backward, length=LARGE_LEN),
        partial(attend_backward, length=SMALL_LEN),
        query_low,
        keys_low,
        values_low,
        lse_rows,
        grad_att_low,
    )
    grad_joint_low = jnp.concatenate([grad_query_low, grad_keys_low, grad_values_low], axis=1)
    grad_joint = jnp.einsum(
        "rd,re->de", first_low, grad_joint_low, preferred_element_type=jnp.float32
    )
    grad_query_add = jnp.sum(grad_query_low.astype(jnp.float32), axis=0)
    grad_value_add = jnp.sum(grad_values_low.astype(jnp.float32), axis=0)
    grad_first = jnp.einsum(
        "re,de->rd", grad_joint_low, joint_back, preferred_element_type=jnp.float32
    )
    grad_stream_norm, grad_gain_one, grad_shift_one = norm_back(
        grad_first, first_hat, first_inv, gain_one_back.astype(jnp.float32)
    )
    grad_stream = grad_mid + grad_stream_norm
    tokens_grad = grad_stream.astype(jnp.bfloat16)
    grad_table = jnp.dot(spread.T, grad_stream, precision=lax.Precision.HIGHEST)
    dp_size = lax.axis_size("dp")
    fsdp_size = lax.axis_size("fsdp")
    group_high = dp_size * 7 // 16
    group_low = dp_size - group_high
    counts = image_counts.astype(jnp.float32)
    share = jnp.where(is_large, counts[1], counts[0]) / (counts[0] + counts[1])
    images = jnp.where(
        is_large,
        group_high * fsdp_size * (ROWS // LARGE_LEN),
        group_low * fsdp_size * (ROWS // SMALL_LEN),
    ).astype(jnp.float32)
    factor = share / images
    grads = (
        grad_joint,
        grad_outproj,
        grad_hidden_w,
        grad_return_w,
        grad_gain_one,
        grad_shift_one,
        grad_query_add,
        grad_value_add,
        grad_output_add,
        grad_gain_two,
        grad_shift_two,
        grad_hidden_add,
        grad_return_add,
        grad_table,
    )
    shares = (
        lax.psum_scatter(
            grads[0].astype(jnp.bfloat16), "fsdp", scatter_dimension=0, tiled=True
        ).astype(jnp.float32),
        lax.psum_scatter(
            grads[1].astype(jnp.bfloat16), "fsdp", scatter_dimension=0, tiled=True
        ).astype(jnp.float32),
        lax.psum_scatter(
            grads[2].astype(jnp.bfloat16), "fsdp", scatter_dimension=0, tiled=True
        ).astype(jnp.float32),
        lax.psum_scatter(
            grads[3].astype(jnp.bfloat16), "fsdp", scatter_dimension=0, tiled=True
        ).astype(jnp.float32),
        lax.psum_scatter(
            grads[4].astype(jnp.bfloat16), "fsdp", scatter_dimension=0, tiled=True
        ).astype(jnp.float32),
        lax.psum_scatter(
            grads[5].astype(jnp.bfloat16), "fsdp", scatter_dimension=0, tiled=True
        ).astype(jnp.float32),
        lax.psum_scatter(
            grads[6].astype(jnp.bfloat16), "fsdp", scatter_dimension=0, tiled=True
        ).astype(jnp.float32),
        lax.psum_scatter(
            grads[7].astype(jnp.bfloat16), "fsdp", scatter_dimension=0, tiled=True
        ).astype(jnp.float32),
        lax.psum_scatter(
            grads[8].astype(jnp.bfloat16), "fsdp", scatter_dimension=0, tiled=True
        ).astype(jnp.float32),
        lax.psum_scatter(
            grads[9].astype(jnp.bfloat16), "fsdp", scatter_dimension=0, tiled=True
        ).astype(jnp.float32),
        lax.psum_scatter(
            grads[10].astype(jnp.bfloat16), "fsdp", scatter_dimension=0, tiled=True
        ).astype(jnp.float32),
        lax.psum_scatter(
            grads[11].astype(jnp.bfloat16), "fsdp", scatter_dimension=0, tiled=True
        ).astype(jnp.float32),
        lax.psum_scatter(
            grads[12].astype(jnp.bfloat16), "fsdp", scatter_dimension=0, tiled=True
        ).astype(jnp.float32),
        lax.psum_scatter(
            grads[13].astype(jnp.bfloat16), "fsdp", scatter_dimension=1, tiled=True
        ).astype(jnp.float32),
    )
    merged = jax.tree.map(
        lambda part: part.astype(jnp.float32),
        lax.psum(shortened(tuple((piece * factor for piece in shares))), "dp"),
    )
    return (
        block_out,
        tokens_grad,
        merged[13],
        merged[4],
        merged[5],
        merged[0],
        merged[6],
        merged[7],
        merged[1],
        merged[8],
        merged[9],
        merged[10],
        merged[2],
        merged[11],
        merged[3],
        merged[12],
    )


def solution(mesh):
    in_specs = (
        P(("dp", "fsdp"), None),
        P(("dp", "fsdp"), None),
        P("dp"),
        P(),
        P(),
        P(None, "fsdp"),
        P("fsdp"),
        P("fsdp"),
        P("fsdp", None),
        P("fsdp"),
        P("fsdp"),
        P("fsdp", None),
        P("fsdp"),
        P("fsdp"),
        P("fsdp"),
        P("fsdp", None),
        P("fsdp"),
        P("fsdp", None),
        P("fsdp"),
    )
    out_specs = (
        P(("dp", "fsdp"), None),
        P(("dp", "fsdp"), None),
        P(None, "fsdp"),
        P("fsdp"),
        P("fsdp"),
        P("fsdp", None),
        P("fsdp"),
        P("fsdp"),
        P("fsdp", None),
        P("fsdp"),
        P("fsdp"),
        P("fsdp"),
        P("fsdp", None),
        P("fsdp"),
        P("fsdp", None),
        P("fsdp"),
    )
    return jax.shard_map(
        per_device, mesh=mesh, in_specs=in_specs, out_specs=out_specs, check_vma=False
    )
```

profile of v0, /device:TPU:0, one launch (start us, length us, event | category | flops | bytes accessed | tf_op | source)
XLA Modules:
  0.0 1341.7 jit_solution(7933301942073396000)
XLA Ops:
  90.6 16.1 %all_gather.48 = bf16[50,1024]{1,0:T(8,128)(2,1)S(1)} all-gather(bf16[50,256]{1,0:T(8,128)(2,1)S(1)} %copy-done.33), channel_id=1, replica_groups=mesh['dp'=8,'fsdp'=4] {'fsdp'}, dimensions={1}, use_global_device_ids=true | all-gather | bytes 128000 | tf_op jit(solution)/shard_map/all_gather | solution.py:158
  114.2 15.8 %all-gather.13.cloned.1.call-done = bf16[1024,3072]{1,0:T(8,128)(2,1)} async-done(((bf16[256,3072]{1,0:T(8,128)(2,1)}), bf16[1024,3072]{1,0:T(8,128)(2,1)}) %all-gather.13.cloned.1.call-update) | async-done | bytes 6291472 | tf_op jit(solution)/shard_map/all_gather | solution.py:145
  130.0 17.1 %fusion.72 = f32[1450,3072]{1,0:T(8,128)} fusion(bf16[1024,3072]{1,0:T(8,128)(2,1)} %all-gather.13.cloned.1.call-done, f32[1450,1024]{1,0:T(8,128)} %copy-done.7, f32[1024]{0:T(1024)S(1)} %bitcast.103, f32[1024]{0:T(1024)S(1)} %bitcast.95, f32[1450]{0:T(1024)S(1)} %add_rsqrt_fusion.1, f32[1450]{0:T(1024)S(1)} %broadcast_multiply_fusion.5), kind=kOutput, calls=%fused_computation.164 | convolution fusion | flops 9130035200 | bytes 30068048 | tf_op jit(solution)/shard_map/dot_general | solution.py:195
  160.3 75.3 %conditional.6 = (f32[1450,16]{0,1:T(8,128)}, bf16[1450,1024]{1,0:T(8,128)(2,1)S(1)}) conditional(s32[]{:T(128)} %convert_element_type.404, (bf16[1450,1024]{1,0:T(8,128)(2,1)}, bf16[1450,1024]{1,0:T(8,128)(2,1)S(1)}, bf16[1450,1024]{1,0:T(8,128)(2,1)}) %tuple.44, (bf16[1450,1024]{1,0:T(8,128)(2,1)}, bf16[1450,1024]{1,0:T(8,128)(2,1)S(1)}, ...), branch_computations={%region_3.6_spmd, %region_6.9_spmd} | conditional | flops 889557632 | bytes 82963216
  175.4 14.4 %multiply_reduce_fusion = (f32[29,16,50]{2,1,0:T(8,128)S(1)}, f32[29,16,50,50]{2,3,1,0:T(8,128)}) fusion(bf16[29,50,16,64]{3,2,1,0:T(8,128)(2,1)} %reshape.397, bf16[29,50,16,64]{3,2,1,0:T(8,128)(2,1)} %reshape.396), kind=kOutput, calls=%fused_computation.2 | convolution fusion | flops 150776800 | bytes 10672000 | tf_op jit(solution)/shard_map/cond/branch_0_fun/nqhd,nkhd->nhqk/dot_general | solution.py:74
  246.5 79.2 %all-gather.17.cloned.1.call-done = bf16[1024,4096]{1,0:T(8,128)(2,1)} async-done(((bf16[256,4096]{1,0:T(8,128)(2,1)}), bf16[1024,4096]{1,0:T(8,128)(2,1)}) %all-gather.17.cloned.1.call-update) | async-done | bytes 8388624 | tf_op jit(solution)/shard_map/all_gather | solution.py:147
  325.7 70.6 %multiply_convert_fusion.4 = (bf16[1450,4096]{1,0:T(8,128)(2,1)}, f32[1450,4096]{1,0:T(8,128)}, f32[1450,4096]{1,0:T(8,128)}) fusion(f32[4096]{0:T(1024)S(1)} %convert_element_type.416, bf16[1024,4096]{1,0:T(8,128)(2,1)} %all-gather.17.cloned.1.call-done, f32[1450,1024]{1,0:T(8,128)} %copy-done.8, f32[1024]{0:T(1024)S(1)} %bitcast.101, ...), kind=kOutput, calls=%fused_computation.59 | convolution fusion | flops 12562892800 | bytes 73755984 | tf_op jit(solution)/shard_map/dot_general | solution.py:216
  396.3 78.7 %all-gather.19.cloned.1.call-done = bf16[4096,1024]{1,0:T(8,128)(2,1)} async-done(((bf16[1024,1024]{1,0:T(8,128)(2,1)}), bf16[4096,1024]{1,0:T(8,128)(2,1)}) %all-gather.19.cloned.1.call-update) | async-done | bytes 8388624 | tf_op jit(solution)/shard_map/all_gather | solution.py:148
  475.0 32.7 %fusion.79 = (bf16[4096]{0:T(1024)(128)(2,1)}, bf16[1450,4096]{1,0:T(8,128)(2,1)}) fusion(f32[1450,4096]{1,0:T(8,128)} %get-tuple-element.140, bf16[1450,1024]{1,0:T(8,128)(2,1)} %param.24, bf16[4096,1024]{1,0:T(8,128)(2,1)} %all-gather.19.cloned.1.call-done, f32[1450,4096]{1,0:T(8,128)} %get-tuple-element.158, f32[4096]{0:T(1024)S(1)} %convert_element_type.416), kind=kOutput, calls=%fused_computation.170 | convolution fusion | flops 12258504704 | bytes 70774784 | tf_op jit(solution)/shard_map/rd,fd->rf/dot_general | solution.py:239
  507.7 22.8 %multiply_reduce_fusion.4 = (bf16[1024]{0:T(1024)(128)(2,1)}, f32[1450]{0:T(1024)S(1)}, f32[1450]{0:T(1024)S(1)}, bf16[1024]{0:T(1024)(128)(2,1)}, f32[1450,1024]{1,0:T(8,128)}) fusion(f32[1450,1024]{1,0:T(8,128)S(1)} %copy-done.9, f32[1450]{0:T(1024)S(1)} %add_rsqrt_fusion, f32[1450]{0:T(1024)S(1)} %broadcast_multiply_fusion.4, f32[1024]{0:T(1024)S(1)} %bitcast.92, ...), kind=kOutput, calls=%fused_computation.81 | convolution fusion | flops 12176840704 | bytes 32176800 | tf_op jit(solution)/shard_map/rf,df->rd/dot_general | solution.py:247
  552.4 154.3 %conditional.7 = (bf16[1450,1024]{1,0:T(8,128)(2,1)S(1)}, bf16[1450,1024]{1,0:T(8,128)(2,1)}, bf16[1450,1024]{1,0:T(8,128)(2,1)}) conditional(s32[]{:T(128)} %convert_element_type.404, (bf16[1450,1024]{1,0:T(8,128)(2,1)}, bf16[1450,1024]{1,0:T(8,128)(2,1)S(1)}, f32[1450,16]{0,1:T(8,128)S(1)}, bf16[1450,1024]{1,0:T(8,128)(2,1)}, ...), branch_computations={%region_13.15_spmd, %region_15.17_spmd} | conditional | flops 2199244032 | bytes 259700960
  583.4 13.5 %subtract_exponential_fusion = f32[29,16,50,50]{2,3,1,0:T(8,128)} fusion(f32[29,16,50]{2,1,0:T(8,128)S(1)} %copy.163, bf16[29,50,16,64]{3,2,1,0:T(8,128)(2,1)} %reshape.405, bf16[29,50,16,64]{3,2,1,0:T(8,128)(2,1)} %reshape.404), kind=kOutput, calls=%fused_computation.30 | convolution fusion | flops 150800000 | bytes 10672000 | tf_op jit(solution)/shard_map/cond/branch_0_fun/nqhd,nkhd->nhqk/dot_general | solution.py:74
  617.7 14.1 %multiply_reduce_fusion.2 = (f32[29,16,50]{2,1,0:T(8,128)S(1)}, f32[29,16,50,50]{2,3,1,0:T(8,128)}) fusion(f32[29,16,50,50]{2,3,1,0:T(8,128)} %subtract_exponential_fusion, bf16[29,50,16,64]{3,2,1,0:T(8,128)(2,1)} %reshape.408, bf16[29,50,16,64]{3,2,1,0:T(8,128)(2,1)} %reshape.407), kind=kOutput, calls=%fused_computation.29 | convolution fusion | flops 150776800 | bytes 15312000 | tf_op jit(solution)/shard_map/cond/branch_0_fun/nqhd,nkhd->nhqk/dot_general | solution.py:105
  706.8 18.2 %convolution_convert_fusion.3 = bf16[1024,3072]{1,0:T(8,128)(2,1)} fusion(bf16[1450,1024]{1,0:T(8,128)(2,1)} %get-tuple-element.93, bf16[1450,1024]{1,0:T(8,128)(2,1)} %get-tuple-element.92, bf16[1450,1024]{1,0:T(8,128)(2,1)S(1)} %get-tuple-element.91, f32[1450,1024]{1,0:T(8,128)} %copy-done.7, f32[1024]{0:T(1024)S(1)} %bitcast.104, f32[1024]{0:T(1024)S(1)} %bitcast.96, ...), kind=kOutput, calls=%fused_computation.94 | convolution fusion | flops 9159907328 | bytes 21159248 | tf_op jit(solution)/shard_map/rd,re->de/dot_general | solution.py:274
  725.7 21.0 %convolution_convert_fusion.1 = bf16[1024,4096]{1,0:T(8,128)(2,1)} fusion(bf16[1450,4096]{1,0:T(8,128)(2,1)} %get-tuple-element.162, f32[1450,1024]{1,0:T(8,128)} %copy-done.8, f32[1024]{0:T(1024)S(1)} %bitcast.102, f32[1024]{0:T(1024)S(1)} %bitcast.94, f32[1450]{0:T(1024)S(1)} %copy-done.32, f32[1450]{0:T(1024)S(1)} %copy-done.28), kind=kOutput, calls=%fused_computation.74 | convolution fusion | flops 12175099904 | bytes 26226000 | tf_op jit(solution)/shard_map/rd,rf->df/dot_general | solution.py:243
  748.6 18.5 %convolution_convert_fusion.2 = bf16[4096,1024]{1,0:T(8,128)(2,1)} fusion(bf16[1450,4096]{1,0:T(8,128)(2,1)} %get-tuple-element.139, bf16[1450,1024]{1,0:T(8,128)(2,1)S(1)} %copy-done.17), kind=kOutput, calls=%fused_computation.75 | convolution fusion | flops 12167675904 | bytes 23236608 | tf_op jit(solution)/shard_map/rf,rd->fd/dot_general | solution.py:235
  783.7 18.3 %multiply_reduce_fusion.5 = (bf16[1024]{0:T(1024)(128)(2,1)S(1)}, f32[1450]{0:T(1024)S(1)}, f32[1450]{0:T(1024)S(1)}, bf16[1024]{0:T(1024)(128)(2,1)S(1)}, f32[1450,1024]{1,0:T(8,128)}) fusion(f32[1450,1024]{1,0:T(8,128)} %copy-done.7, f32[1450]{0:T(1024)S(1)} %copy-done.30, f32[1450]{0:T(1024)S(1)} %copy-done.26, f32[1024]{0:T(1024)S(1)} %bitcast.97, ...), kind=kOutput, calls=%fused_computation.82 | convolution fusion | flops 9162696704 | bytes 27110048 | tf_op jit(solution)/shard_map/re,de->rd/dot_general | solution.py:279
  802.0 21.2 %all-reduce.11 = (bf16[1024]{0:T(1024)(128)(2,1)S(1)}, bf16[1024]{0:T(1024)(128)(2,1)S(1)}, bf16[1024]{0:T(1024)(128)(2,1)S(1)}, bf16[1024]{0:T(1024)(128)(2,1)S...) all-reduce(bf16[1024]{0:T(1024)(128)(2,1)S(1)} %get-tuple-element.1, ...), channel_id=3, replica_groups=mesh['dp'=8,'fsdp'=4] {'fsdp'}, use_global_device_ids=true, to_apply=%region_22.23.clone | all-reduce | flops 12288 | bytes 49152
  839.2 58.6 %reduce-scatter.8.cloned.1.call-done = bf16[256,3072]{1,0:T(8,128)(2,1)} async-done(((bf16[1024,3072]{1,0:T(8,128)(2,1)}), bf16[256,3072]{1,0:T(8,128)(2,1)}) %reduce-scatter.8.cloned.1.call-update) | async-done | bytes 1572880 | tf_op jit(solution)/shard_map/reduce_scatter | solution.py:317
  900.6 144.6 %reduce-scatter.12.cloned.1.call-done = bf16[256,4096]{1,0:T(8,128)(2,1)} async-done(((bf16[1024,4096]{1,0:T(8,128)(2,1)}), bf16[256,4096]{1,0:T(8,128)(2,1)}) %reduce-scatter.12.cloned.1.call-update) | async-done | bytes 2097168 | tf_op jit(solution)/shard_map/reduce_scatter | solution.py:323
  1048.6 144.4 %reduce-scatter.14.cloned.1.call-done = bf16[1024,1024]{1,0:T(8,128)(2,1)} async-done(((bf16[4096,1024]{1,0:T(8,128)(2,1)}), bf16[1024,1024]{1,0:T(8,128)(2,1)}) %reduce-scatter.14.cloned.1.call-update) | async-done | bytes 2097168 | tf_op jit(solution)/shard_map/reduce_scatter | solution.py:326
  1196.4 19.1 %add_convert_fusion.1 = bf16[1450,1024]{1,0:T(8,128)(2,1)} fusion(f32[1450,1024]{1,0:T(8,128)} %copy-done.8, bf16[1450,4096]{1,0:T(8,128)(2,1)} %get-tuple-element.139, bf16[4096,1024]{1,0:T(8,128)(2,1)} %all-gather.19.cloned.1.call-done, f32[1024]{0:T(1024)S(1)} %bitcast.106), kind=kOutput, calls=%fused_computation.87 | convolution fusion | flops 12167936000 | bytes 29179904 | tf_op jit(solution)/shard_map/dot_general | solution.py:221
  1216.3 25.7 %all-reduce.9 = (bf16[50,256]{1,0:T(8,128)(2,1)S(1)}, bf16[256]{0:T(256)(128)(2,1)S(1)}, bf16[256]{0:T(256)(128)(2,1)S(1)}, bf16[256]{0:T(256)(128)(2,1)S(1)}, b...) all-reduce(bf16[50,256]{1,0:T(8,128)(2,1)S(1)} %multiply_convert_fu, ...), channel_id=1, replica_groups=mesh['dp'=8,'fsdp'=4] {'dp'}, use_global_device_ids=true, to_apply=%region_20.21 | all-reduce | flops 15872 | bytes 63488 | tf_op jit(solution)/shard_map/psum | solution.py:362
  1247.7 75.9 %all-reduce.14.cloned.1.call-done = (bf16[256,3072]{1,0:T(8,128)(2,1)}, bf16[256,1024]{1,0:T(8,128)(2,1)}, bf16[256,4096]{1,0:T(8,128)(2,1)}, bf16[1024,1024]{1,0:T(8,128)(2,1)}) async-done(((bf16[256,3072]{1,0:T(8,128)(2,1)}, bf16[256,1024]{1,0:T(8,128)(2,1)}, bf16[256,4096]{1,0:T(8,128)(2,1)}, bf16[1024,1024]{1,0:T(8,128)(2,1)}), (bf16[256,3072]{1,0:T(8,128)(2,1)}, bf16[256,1024]{1,0:T(8,128)(2,1)}, ...) | async-done | bytes 6291472 | tf_op jit(solution)/shard_map/psum | solution.py:362
  (245 shorter events, 359.2 us)
Async XLA Ops:
  7.3 71.3 %copy-start.46 = (bf16[1024]{0:T(1024)(128)(2,1)S(1)}, bf16[1024]{0:T(1024)(128)(2,1)}, u32[]{:S(2)}) copy-start(bf16[1024]{0:T(1024)(128)(2,1)} %param.39) | copy-start | bytes 6148
  7.3 83.3 %copy-start.33 = (bf16[50,256]{1,0:T(8,128)(2,1)S(1)}, bf16[50,256]{1,0:T(8,128)(2,1)}, u32[]{:S(2)}) copy-start(bf16[50,256]{1,0:T(8,128)(2,1)} %param.28) | copy-start | bytes 76804
  7.3 99.5 %copy-start.41 = (s32[145,4]{0,1:T(4,128)S(1)}, s32[145,4]{0,1:T(4,128)}, u32[]{:S(2)}) copy-start(s32[145,4]{0,1:T(4,128)} %param.27) | copy-start | bytes 6964
  7.3 100.5 %copy-start.18 = (bf16[1450,1024]{1,0:T(8,128)(2,1)S(1)}, bf16[1450,1024]{1,0:T(8,128)(2,1)}, u32[]{:S(2)}) copy-start(bf16[1450,1024]{1,0:T(8,128)(2,1)} %param.23) | copy-start | bytes 8908804
  7.3 122.7 %all-gather.13.cloned.1.call-start = ((), (), s32[]{:S(2)}) async-start(), calls=%async_computation.5 | async-start | bytes 7864320 | tf_op jit(solution)/shard_map/all_gather | solution.py:145
  8.0 227.7 %all-gather.15.cloned.1.call-start = ((), (), s32[]{:S(2)}) async-start(), calls=%async_computation.6 | async-start | bytes 2621440 | tf_op jit(solution)/shard_map/all_gather | solution.py:146
  8.8 316.9 %all-gather.17.cloned.1.call-start = ((), (), s32[]{:S(2)}) async-start(), calls=%async_computation.7 | async-start | bytes 10485760 | tf_op jit(solution)/shard_map/all_gather | solution.py:147
  9.5 465.5 %all-gather.19.cloned.1.call-start = ((), (), s32[]{:S(2)}) async-start(), calls=%async_computation.8 | async-start | bytes 10485760 | tf_op jit(solution)/shard_map/all_gather | solution.py:148
  10.1 827.2 %reduce-scatter.10.cloned.1.call-start = ((), (), s32[]{:S(2)}) async-start(), calls=%async_computation.11 | async-start | bytes 2621440 | tf_op jit(solution)/shard_map/reduce_scatter | solution.py:320
  23.7 302.0 %copy-start.42 = (f32[4,1,256]{2,1,0:T(1,128)}, f32[4,1,256]{2,1,0:T(1,128)S(1)}, u32[]{:S(2)}) copy-start(f32[4,1,256]{2,1,0:T(1,128)S(1)} %convert_element_type.486) | copy-start | bytes 12292
  31.4 499.1 %copy-start.34 = (f32[4,1,256]{2,1,0:T(1,128)}, f32[4,1,256]{2,1,0:T(1,128)S(1)}, u32[]{:S(2)}) copy-start(f32[4,1,256]{2,1,0:T(1,128)S(1)} %convert_element_type.485) | copy-start | bytes 12292
  69.7 60.2 %copy-start.44 = (f32[4,1,256]{2,1,0:T(1,128)}, f32[4,1,256]{2,1,0:T(1,128)S(1)}, u32[]{:S(2)}) copy-start(f32[4,1,256]{2,1,0:T(1,128)S(1)} %convert_element_type.481) | copy-start | bytes 12292
  78.4 51.6 %copy-start.36 = (f32[4,1,256]{2,1,0:T(1,128)}, f32[4,1,256]{2,1,0:T(1,128)S(1)}, u32[]{:S(2)}) copy-start(f32[4,1,256]{2,1,0:T(1,128)S(1)} %convert_element_type.480) | copy-start | bytes 12292
  243.2 287.2 %copy-start.27 = (f32[1450]{0:T(1024)}, f32[1450]{0:T(1024)S(1)}, u32[]{:S(2)}) copy-start(f32[1450]{0:T(1024)S(1)} %broadcast_multiply_fusion.4) | copy-start | bytes 17404
  246.5 284.0 %copy-start.31 = (f32[1450]{0:T(1024)}, f32[1450]{0:T(1024)S(1)}, u32[]{:S(2)}) copy-start(f32[1450]{0:T(1024)S(1)} %add_rsqrt_fusion) | copy-start | bytes 17404
  544.0 353.8 %reduce-scatter.8.cloned.1.call-start = ((), (), s32[]{:S(2)}) async-start(), calls=%async_computation.10 | async-start | bytes 7864320 | tf_op jit(solution)/shard_map/reduce_scatter | solution.py:317
  552.4 154.4 %copy-start.26 = (f32[1450]{0:T(1024)S(1)}, f32[1450]{0:T(1024)}, u32[]{:S(2)}) copy-start(f32[1450]{0:T(1024)} %copy-done.25) | copy-start | bytes 17404
  552.4 154.4 %copy-start.30 = (f32[1450]{0:T(1024)S(1)}, f32[1450]{0:T(1024)}, u32[]{:S(2)}) copy-start(f32[1450]{0:T(1024)} %copy-done.29) | copy-start | bytes 17404
  552.4 154.4 %copy-start.37 = (f32[4,1,256]{2,1,0:T(1,128)S(1)}, f32[4,1,256]{2,1,0:T(1,128)}, u32[]{:S(2)}) copy-start(f32[4,1,256]{2,1,0:T(1,128)} %copy-done.36) | copy-start | bytes 12292
  552.4 154.4 %copy-start.45 = (f32[4,1,256]{2,1,0:T(1,128)S(1)}, f32[4,1,256]{2,1,0:T(1,128)}, u32[]{:S(2)}) copy-start(f32[4,1,256]{2,1,0:T(1,128)} %copy-done.44) | copy-start | bytes 12292
  725.1 320.2 %reduce-scatter.12.cloned.1.call-start = ((), (), s32[]{:S(2)}) async-start(), calls=%async_computation.12 | async-start | bytes 10485760 | tf_op jit(solution)/shard_map/reduce_scatter | solution.py:323
  746.8 446.2 %reduce-scatter.14.cloned.1.call-start = ((), (), s32[]{:S(2)}) async-start(), calls=%async_computation.13 | async-start | bytes 10485760 | tf_op jit(solution)/shard_map/reduce_scatter | solution.py:326
  767.1 448.4 %reduce-scatter.6.cloned.1.call-start = ((), (), s32[]{:S(2)}) async-start(), calls=%async_computation.9 | async-start | bytes 143360 | tf_op jit(solution)/shard_map/reduce_scatter | solution.py:356
  837.2 486.4 %all-reduce.14.cloned.1.call-start = ((), (), s32[]{:S(2)}) async-start(), calls=%async_computation.14 | async-start | bytes 12582912 | tf_op jit(solution)/shard_map/psum | solution.py:362
  (41 other events, 356.6 us)
Sparse Core Ops, SparseCore 0:
  9.7 120.2 all-gather.12
  131.5 44.1 all-gather.14
  177.3 148.3 all-gather.16
  327.1 147.8 all-gather.18
  544.1 42.0 reduce-scatter.9
  725.2 172.5 reduce-scatter.7
  900.3 144.9 reduce-scatter.11
  1047.8 145.1 reduce-scatter.13
  1195.3 19.8 reduce-scatter.5
  1219.9 103.7 all-reduce.13
where the time goes:
time: 1350 us; the launch traced here: 1340 us
  waiting for transfers between devices  600 us (44%)
  matrix products  347 us (26%)
  blocking collectives  150 us (11%)
  local copies, waits for them, and re-layouts  124 us (9%)
  other arithmetic  78.1 us (6%)
  loops' own time  22.1 us (2%)
  between operations  20 us (1%)
    reduce_scatter x1, waiting for transfers between devices, per_device(): lax.psum_scatter(grads[2].astype(jnp.bfloat16), 'fsdp', scatter_dimension...  145 us
    reduce_scatter x1, waiting for transfers between devices, per_device(): lax.psum_scatter(grads[3].astype(jnp.bfloat16), 'fsdp', scatter_dimension...  144 us
    all_gather x1, waiting for transfers between devices, per_device(): lax.all_gather(hidden_weight, 'fsdp', axis=0, tiled=True)  79.2 us
    all_gather x1, waiting for transfers between devices, per_device(): lax.all_gather(return_weight, 'fsdp', axis=0, tiled=True)  78.7 us
    psum x1, waiting for transfers between devices, per_device(): lax.psum(shortened(tuple((piece * factor for piece in shares))), 'dp')  75.9 us
    dot_general x1, matrix products, per_device(): jnp.dot(second_low, hidden_full, preferred_element_type=jnp.float32)  70.6 us
    reduce_scatter x1, waiting for transfers between devices, per_device(): lax.psum_scatter(grads[0].astype(jnp.bfloat16), 'fsdp', scatter_dimension...  58.6 us
    dot_general x1, matrix products, per_device(): jnp.einsum('rd,fd->rf', output_grad, return_back, preferred_element_type=...  32.7 us
  transfers between devices with their start and end apart: 10, of which 7 were waited for; matrix products, arithmetic and copies ran while one was open for 34% of the time, Pallas kernels for 0%

commit v1 on v0

--- a/solution.py
+++ b/solution.py
@@ -14,6 +14,19 @@
 LARGE_LEN = 145
 ROWS = 1450
 EPS = 1e-06
+
+
+def gather_around(x, axis, dim):
+    ways = lax.axis_size(axis)
+    up = [(d, (d + 1) % ways) for d in range(ways)]
+    down = [(d, (d - 1) % ways) for d in range(ways)]
+    earlier, later = ([x], [x])
+    for _ in range(ways // 2):
+        earlier.append(lax.ppermute(earlier[-1], axis, up))
+    for _ in range((ways - 1) // 2):
+        later.append(lax.ppermute(later[-1], axis, down))
+    line = jnp.concatenate([*earlier[::-1], *later[1:]], axis=dim)
+    return jnp.roll(line, (lax.axis_index(axis) - ways // 2) * x.shape[dim], axis=dim)
 
 
 def shortened(value):
@@ -145,7 +158,7 @@
         lax.all_gather(input_proj, "fsdp", axis=0, tiled=True),
         lax.all_gather(output_proj, "fsdp", axis=0, tiled=True),
         lax.all_gather(hidden_weight, "fsdp", axis=0, tiled=True),
-        lax.all_gather(return_weight, "fsdp", axis=0, tiled=True),
+        gather_around(return_weight, "fsdp", 0),
         lax.all_gather(first_gain, "fsdp", axis=0, tiled=True),
         lax.all_gather(first_shift, "fsdp", axis=0, tiled=True),
         lax.all_gather(query_bias, "fsdp", axis=0, tiled=True),

time: 1350 us -> 1450 us (1.074)
  blocking collectives: 150 us -> 299 us
  waiting for transfers between devices: 600 us -> 515 us
  local copies, waits for them, and re-layouts: 124 us -> 146 us
    all_gather x1, blocking collectives: 7.88 us -> 157 us  [per_device(): lax.all_gather(return_bias, 'fsdp', axis=0, tiled=True)]
    reduce_scatter x1, waiting for transfers between devices: 145 us -> 47.1 us  [per_device(): lax.psum_scatter(grads[2].astype(jnp.bfloat16), 'fsdp', scatter_dimension...]
    ppermute x0 -> x3, waiting for transfers between devices: none -> 72.6 us  [the longest x2 72.6 us: gather_around(): earlier.append(lax.ppermute(earlier[-1], axis, up))]
    reduce_scatter x1, waiting for transfers between devices: 58.6 us -> 0.01 us  [per_device(): lax.psum_scatter(grads[0].astype(jnp.bfloat16), 'fsdp', scatter_dimension...]
    unnamed x113 -> x122, local copies, waits for them, and re-layouts: 10.9 us -> 30.3 us
  transfers between devices with their start and end apart: 10 -> 13, of which waited for: 7 -> 7; matrix products, arithmetic and copies ran while one was open for 34% -> 33% of each run, Pallas kernels for 0% -> 0%
where the time goes in v1:
time: 1450 us; the launch traced here: 1440 us
  waiting for transfers between devices  515 us (36%)
  matrix products  347 us (24%)
  blocking collectives  299 us (21%)
  local copies, waits for them, and re-layouts  146 us (10%)
  other arithmetic  78.2 us (5%)
  loops' own time  22.2 us (2%)
  between operations  19.7 us (1%)
    all_gather x1, blocking collectives, per_device(): lax.all_gather(return_bias, 'fsdp', axis=0, tiled=True)  157 us
    reduce_scatter x1, waiting for transfers between devices, per_device(): lax.psum_scatter(grads[3].astype(jnp.bfloat16), 'fsdp', scatter_dimension...  144 us
    all_gather x1, waiting for transfers between devices, per_device(): lax.all_gather(hidden_weight, 'fsdp', axis=0, tiled=True)  79.1 us
    all_gather x1, waiting for transfers between devices, per_device(): lax.all_gather(return_weight, 'fsdp', axis=0, tiled=True)  78.7 us
    psum x1, waiting for transfers between devices, per_device(): lax.psum(shortened(tuple((piece * factor for piece in shares))), 'dp')  75.8 us
    ppermute x2, waiting for transfers between devices, gather_around(): earlier.append(lax.ppermute(earlier[-1], axis, up))  72.6 us
    dot_general x1, matrix products, per_device(): jnp.dot(second_low, hidden_full, preferred_element_type=jnp.float32)  70.6 us
    reduce_scatter x1, waiting for transfers between devices, per_device(): lax.psum_scatter(grads[2].astype(jnp.bfloat16), 'fsdp', scatter_dimension...  47.1 us
  transfers between devices with their start and end apart: 13, of which 7 were waited for; matrix products, arithmetic and copies ran while one was open for 33% of the time, Pallas kernels for 0%

profile of v1, /device:TPU:0, one launch (start us, length us, event | category | flops | bytes accessed | tf_op | source)
XLA Modules:
  0.0 1441.5 jit_solution(767518981834758422)
XLA Ops:
  90.6 16.1 %all_gather.47 = bf16[50,1024]{1,0:T(8,128)(2,1)S(1)} all-gather(bf16[50,256]{1,0:T(8,128)(2,1)S(1)} %copy-done.34), channel_id=1, replica_groups=mesh['dp'=8,'fsdp'=4] {'fsdp'}, dimensions={1}, use_global_device_ids=true | all-gather | bytes 128000 | tf_op jit(solution)/shard_map/all_gather | solution.py:171
  114.3 15.7 %all-gather.13.cloned.1.call-done = bf16[1024,3072]{1,0:T(8,128)(2,1)} async-done(((bf16[256,3072]{1,0:T(8,128)(2,1)}), bf16[1024,3072]{1,0:T(8,128)(2,1)}) %all-gather.13.cloned.1.call-update) | async-done | bytes 6291472 | tf_op jit(solution)/shard_map/all_gather | solution.py:158
  130.0 17.2 %fusion.77 = f32[1450,3072]{1,0:T(8,128)} fusion(bf16[1024,3072]{1,0:T(8,128)(2,1)} %all-gather.13.cloned.1.call-done, f32[1450,1024]{1,0:T(8,128)} %copy-done.7, f32[1024]{0:T(1024)S(1)} %bitcast.102, f32[1024]{0:T(1024)S(1)} %bitcast.94, f32[1450]{0:T(1024)S(1)} %add_rsqrt_fusion.1, f32[1450]{0:T(1024)S(1)} %broadcast_multiply_fusion.5), kind=kOutput, calls=%fused_computation.175 | convolution fusion | flops 9130035200 | bytes 30068048 | tf_op jit(solution)/shard_map/dot_general | solution.py:208
  160.4 75.4 %conditional.6 = (f32[1450,16]{0,1:T(8,128)}, bf16[1450,1024]{1,0:T(8,128)(2,1)S(1)}) conditional(s32[]{:T(128)} %convert_element_type.404, (bf16[1450,1024]{1,0:T(8,128)(2,1)}, bf16[1450,1024]{1,0:T(8,128)(2,1)S(1)}, bf16[1450,1024]{1,0:T(8,128)(2,1)}) %tuple.44, (bf16[1450,1024]{1,0:T(8,128)(2,1)}, bf16[1450,1024]{1,0:T(8,128)(2,1)S(1)}, ...), branch_computations={%region_3.6_spmd, %region_6.9_spmd} | conditional | flops 889557632 | bytes 82963216
  175.7 14.3 multiply_reduce_fusion
  246.5 79.1 %all-gather.17.cloned.1.call-done = bf16[1024,4096]{1,0:T(8,128)(2,1)} async-done(((bf16[256,4096]{1,0:T(8,128)(2,1)}), bf16[1024,4096]{1,0:T(8,128)(2,1)}) %all-gather.17.cloned.1.call-update) | async-done | bytes 8388624 | tf_op jit(solution)/shard_map/all_gather | solution.py:160
  325.7 70.6 %multiply_convert_fusion.4 = (bf16[1450,4096]{1,0:T(8,128)(2,1)}, f32[1450,4096]{1,0:T(8,128)}, f32[1450,4096]{1,0:T(8,128)}) fusion(f32[4096]{0:T(1024)S(1)} %convert_element_type.416, bf16[1024,4096]{1,0:T(8,128)(2,1)} %all-gather.17.cloned.1.call-done, f32[1450,1024]{1,0:T(8,128)} %copy-done.8, f32[1024]{0:T(1024)S(1)} %bitcast.100, ...), kind=kOutput, calls=%fused_computation.59 | convolution fusion | flops 12562892800 | bytes 73755984 | tf_op jit(solution)/shard_map/dot_general | solution.py:229
  396.3 78.7 %all-gather.19.cloned.1.call-done = bf16[4096,1024]{1,0:T(8,128)(2,1)} async-done(((bf16[1024,1024]{1,0:T(8,128)(2,1)}), bf16[4096,1024]{1,0:T(8,128)(2,1)}) %all-gather.19.cloned.1.call-update) | async-done | bytes 8388624 | tf_op jit(solution)/shard_map/all_gather | solution.py:242
  475.0 32.7 %fusion.84 = (bf16[4096]{0:T(1024)(128)(2,1)}, bf16[1450,4096]{1,0:T(8,128)(2,1)}) fusion(f32[1450,4096]{1,0:T(8,128)} %get-tuple-element.140, bf16[1450,1024]{1,0:T(8,128)(2,1)} %param.24, bf16[4096,1024]{1,0:T(8,128)(2,1)} %all-gather.19.cloned.1.call-done, f32[1450,4096]{1,0:T(8,128)} %get-tuple-element.158, f32[4096]{0:T(1024)S(1)} %convert_element_type.416), kind=kOutput, calls=%fused_computation.181 | convolution fusion | flops 12258504704 | bytes 70774784 | tf_op jit(solution)/shard_map/rd,fd->rf/dot_general | solution.py:252
  507.7 22.7 %multiply_reduce_fusion.4 = (bf16[1024]{0:T(1024)(128)(2,1)}, f32[1450]{0:T(1024)S(1)}, f32[1450]{0:T(1024)S(1)}, bf16[1024]{0:T(1024)(128)(2,1)}, f32[1450,1024]{1,0:T(8,128)}) fusion(f32[1450,1024]{1,0:T(8,128)S(1)} %copy-done.9, f32[1450]{0:T(1024)S(1)} %add_rsqrt_fusion, f32[1450]{0:T(1024)S(1)} %broadcast_multiply_fusion.4, f32[1024]{0:T(1024)S(1)} %bitcast.91, ...), kind=kOutput, calls=%fused_computation.83 | convolution fusion | flops 12176840704 | bytes 32176800 | tf_op jit(solution)/shard_map/rf,df->rd/dot_general | solution.py:260
  552.4 154.3 %conditional.7 = (bf16[1450,1024]{1,0:T(8,128)(2,1)S(1)}, bf16[1450,1024]{1,0:T(8,128)(2,1)}, bf16[1450,1024]{1,0:T(8,128)(2,1)}) conditional(s32[]{:T(128)} %convert_element_type.404, (bf16[1450,1024]{1,0:T(8,128)(2,1)}, bf16[1450,1024]{1,0:T(8,128)(2,1)S(1)}, f32[1450,16]{0,1:T(8,128)S(1)}, bf16[1450,1024]{1,0:T(8,128)(2,1)}, ...), branch_computations={%region_13.15_spmd, %region_15.17_spmd} | conditional | flops 2199244032 | bytes 259700960
  617.6 14.3 multiply_reduce_fusion.2
  706.8 18.2 %convolution_convert_fusion.3 = bf16[1024,3072]{1,0:T(8,128)(2,1)} fusion(bf16[1450,1024]{1,0:T(8,128)(2,1)} %get-tuple-element.93, bf16[1450,1024]{1,0:T(8,128)(2,1)} %get-tuple-element.92, bf16[1450,1024]{1,0:T(8,128)(2,1)S(1)} %get-tuple-element.91, f32[1450,1024]{1,0:T(8,128)} %copy-done.7, f32[1024]{0:T(1024)S(1)} %bitcast.103, f32[1024]{0:T(1024)S(1)} %bitcast.95, ...), kind=kOutput, calls=%fused_computation.96 | convolution fusion | flops 9159907328 | bytes 21159248 | tf_op jit(solution)/shard_map/rd,re->de/dot_general | solution.py:287
  725.7 21.0 %convolution_convert_fusion.1 = bf16[1024,4096]{1,0:T(8,128)(2,1)} fusion(bf16[1450,4096]{1,0:T(8,128)(2,1)} %get-tuple-element.162, f32[1450,1024]{1,0:T(8,128)} %copy-done.8, f32[1024]{0:T(1024)S(1)} %bitcast.101, f32[1024]{0:T(1024)S(1)} %bitcast.93, f32[1450]{0:T(1024)S(1)} %copy-done.33, f32[1450]{0:T(1024)S(1)} %copy-done.29), kind=kOutput, calls=%fused_computation.76 | convolution fusion | flops 12175099904 | bytes 26226000 | tf_op jit(solution)/shard_map/rd,rf->df/dot_general | solution.py:256
  748.5 18.4 %convolution_convert_fusion.2 = bf16[4096,1024]{1,0:T(8,128)(2,1)} fusion(bf16[1450,4096]{1,0:T(8,128)(2,1)} %get-tuple-element.139, bf16[1450,1024]{1,0:T(8,128)(2,1)S(1)} %copy-done.18), kind=kOutput, calls=%fused_computation.77 | convolution fusion | flops 12167675904 | bytes 23236608 | tf_op jit(solution)/shard_map/rf,rd->fd/dot_general | solution.py:248
  768.5 72.6 %collective-permute-done = bf16[1024,1024]{1,0:T(8,128)(2,1)} collective-permute-done((bf16[1024,1024]{1,0:T(8,128)(2,1)S(1)}, bf16[1024,1024]{1,0:T(8,128)(2,1)}, u32[]{:S(2)}, u32[]{:S(2)}) %collective-permute-start) | collective-permute-done | bytes 2097184 | tf_op jit(solution)/shard_map/ppermute | solution.py:25
  859.5 156.6 %all-gather.7 = bf16[4,1,256]{2,1,0:T(2,128)(2,1)S(1)} all-gather(bf16[1,1,256]{2,1,0:T(2,128)(2,1)S(1)} %reshape.432), channel_id=1, replica_groups=mesh['dp'=8,'fsdp'=4] {'fsdp'}, dimensions={0}, use_global_device_ids=true | all-gather | bytes 2560 | tf_op jit(solution)/shard_map/all_gather | solution.py:170
  1040.9 18.3 %multiply_reduce_fusion.5 = (bf16[1024]{0:T(1024)(128)(2,1)S(1)}, f32[1450]{0:T(1024)S(1)}, f32[1450]{0:T(1024)S(1)}, bf16[1024]{0:T(1024)(128)(2,1)S(1)}, f32[1450,1024]{1,0:T(8,128)}) fusion(f32[1450,1024]{1,0:T(8,128)} %copy-done.7, f32[1450]{0:T(1024)S(1)} %copy-done.31, f32[1450]{0:T(1024)S(1)} %copy-done.27, f32[1024]{0:T(1024)S(1)} %bitcast.96, ...), kind=kOutput, calls=%fused_computation.84 | convolution fusion | flops 9162696704 | bytes 27110048 | tf_op jit(solution)/shard_map/re,de->rd/dot_general | solution.py:292
  1059.2 20.8 %all-reduce.11 = (bf16[1024]{0:T(1024)(128)(2,1)S(1)}, bf16[1024]{0:T(1024)(128)(2,1)S(1)}, bf16[1024]{0:T(1024)(128)(2,1)S(1)}, bf16[1024]{0:T(1024)(128)(2,1)S...) all-reduce(bf16[1024]{0:T(1024)(128)(2,1)S(1)} %get-tuple-element.1, ...), channel_id=3, replica_groups=mesh['dp'=8,'fsdp'=4] {'fsdp'}, use_global_device_ids=true, to_apply=%region_22.23.clone | all-reduce | flops 12288 | bytes 49152
  1099.1 47.1 %reduce-scatter.12.cloned.1.call-done = bf16[256,4096]{1,0:T(8,128)(2,1)} async-done(((bf16[1024,4096]{1,0:T(8,128)(2,1)}), bf16[256,4096]{1,0:T(8,128)(2,1)}) %reduce-scatter.12.cloned.1.call-update) | async-done | bytes 2097168 | tf_op jit(solution)/shard_map/reduce_scatter | solution.py:336
  1149.5 143.8 %reduce-scatter.14.cloned.1.call-done = bf16[1024,1024]{1,0:T(8,128)(2,1)} async-done(((bf16[4096,1024]{1,0:T(8,128)(2,1)}), bf16[1024,1024]{1,0:T(8,128)(2,1)}) %reduce-scatter.14.cloned.1.call-update) | async-done | bytes 2097168 | tf_op jit(solution)/shard_map/reduce_scatter | solution.py:339
  1296.7 19.1 %add_convert_fusion.1 = bf16[1450,1024]{1,0:T(8,128)(2,1)} fusion(f32[1450,1024]{1,0:T(8,128)} %copy-done.8, bf16[1450,4096]{1,0:T(8,128)(2,1)} %get-tuple-element.139, bf16[8192,1024]{1,0:T(8,128)(2,1)} %constant_dynamic-update-slice_fusion, s32[]{:T(128)S(6)} %select_n.212, f32[1024]{0:T(1024)S(1)} %bitcast.104), kind=kOutput, calls=%fused_computation.89 | convolution fusion | flops 12167936000 | bytes 29253636 | tf_op jit(solution)/shard_map/dot_general | solution.py:234
  1316.5 25.7 %all-reduce.9 = (bf16[50,256]{1,0:T(8,128)(2,1)S(1)}, bf16[256]{0:T(256)(128)(2,1)S(1)}, bf16[256]{0:T(256)(128)(2,1)S(1)}, bf16[256]{0:T(256)(128)(2,1)S(1)}, b...) all-reduce(bf16[50,256]{1,0:T(8,128)(2,1)S(1)} %multiply_convert_fu, ...), channel_id=1, replica_groups=mesh['dp'=8,'fsdp'=4] {'dp'}, use_global_device_ids=true, to_apply=%region_20.21 | all-reduce | flops 15872 | bytes 63488 | tf_op jit(solution)/shard_map/psum | solution.py:375
  1348.0 75.8 %all-reduce.14.cloned.1.call-done = (bf16[256,3072]{1,0:T(8,128)(2,1)}, bf16[256,1024]{1,0:T(8,128)(2,1)}, bf16[256,4096]{1,0:T(8,128)(2,1)}, bf16[1024,1024]{1,0:T(8,128)(2,1)}) async-done(((bf16[256,3072]{1,0:T(8,128)(2,1)}, bf16[256,1024]{1,0:T(8,128)(2,1)}, bf16[256,4096]{1,0:T(8,128)(2,1)}, bf16[1024,1024]{1,0:T(8,128)(2,1)}), (bf16[256,3072]{1,0:T(8,128)(2,1)}, bf16[256,1024]{1,0:T(8,128)(2,1)}, ...) | async-done | bytes 6291472 | tf_op jit(solution)/shard_map/psum | solution.py:375
  (261 shorter events, 401.1 us)
Async XLA Ops:
  7.3 99.5 %copy-start.42 = (s32[145,4]{0,1:T(4,128)S(1)}, s32[145,4]{0,1:T(4,128)}, u32[]{:S(2)}) copy-start(s32[145,4]{0,1:T(4,128)} %param.27) | copy-start | bytes 6964
  7.3 100.5 %copy-start.19 = (bf16[1450,1024]{1,0:T(8,128)(2,1)S(1)}, bf16[1450,1024]{1,0:T(8,128)(2,1)}, u32[]{:S(2)}) copy-start(bf16[1450,1024]{1,0:T(8,128)(2,1)} %param.23) | copy-start | bytes 8908804
  7.3 122.7 %all-gather.13.cloned.1.call-start = ((), (), s32[]{:S(2)}) async-start(), calls=%async_computation.5 | async-start | bytes 7864320 | tf_op jit(solution)/shard_map/all_gather | solution.py:158
  8.0 227.7 %all-gather.15.cloned.1.call-start = ((), (), s32[]{:S(2)}) async-start(), calls=%async_computation.6 | async-start | bytes 2621440 | tf_op jit(solution)/shard_map/all_gather | solution.py:159
  8.8 316.9 %all-gather.17.cloned.1.call-start = ((), (), s32[]{:S(2)}) async-start(), calls=%async_computation.7 | async-start | bytes 10485760 | tf_op jit(solution)/shard_map/all_gather | solution.py:160
  9.5 465.5 %all-gather.19.cloned.1.call-start = ((), (), s32[]{:S(2)}) async-start(), calls=%async_computation.8 | async-start | bytes 10485760 | tf_op jit(solution)/shard_map/all_gather | solution.py:242
  10.1 1084.1 %reduce-scatter.10.cloned.1.call-start = ((), (), s32[]{:S(2)}) async-start(), calls=%async_computation.11 | async-start | bytes 2621440 | tf_op jit(solution)/shard_map/reduce_scatter | solution.py:333
  23.7 302.0 %copy-start.43 = (f32[4,1,256]{2,1,0:T(1,128)}, f32[4,1,256]{2,1,0:T(1,128)S(1)}, u32[]{:S(2)}) copy-start(f32[4,1,256]{2,1,0:T(1,128)S(1)} %convert_element_type.486) | copy-start | bytes 12292
  31.4 499.1 %copy-start.35 = (f32[4,1,256]{2,1,0:T(1,128)}, f32[4,1,256]{2,1,0:T(1,128)S(1)}, u32[]{:S(2)}) copy-start(f32[4,1,256]{2,1,0:T(1,128)S(1)} %convert_element_type.485) | copy-start | bytes 12292
  243.3 287.1 %copy-start.28 = (f32[1450]{0:T(1024)}, f32[1450]{0:T(1024)S(1)}, u32[]{:S(2)}) copy-start(f32[1450]{0:T(1024)S(1)} %broadcast_multiply_fusion.4) | copy-start | bytes 17404
  246.5 283.9 %copy-start.32 = (f32[1450]{0:T(1024)}, f32[1450]{0:T(1024)S(1)}, u32[]{:S(2)}) copy-start(f32[1450]{0:T(1024)S(1)} %add_rsqrt_fusion) | copy-start | bytes 17404
  543.9 552.3 %reduce-scatter.8.cloned.1.call-start = ((), (), s32[]{:S(2)}) async-start(), calls=%async_computation.10 | async-start | bytes 7864320 | tf_op jit(solution)/shard_map/reduce_scatter | solution.py:330
  552.4 154.4 %copy-start.27 = (f32[1450]{0:T(1024)S(1)}, f32[1450]{0:T(1024)}, u32[]{:S(2)}) copy-start(f32[1450]{0:T(1024)} %copy-done.26) | copy-start | bytes 17404
  552.4 154.4 %copy-start.31 = (f32[1450]{0:T(1024)S(1)}, f32[1450]{0:T(1024)}, u32[]{:S(2)}) copy-start(f32[1450]{0:T(1024)} %copy-done.30) | copy-start | bytes 17404
  552.4 154.4 %copy-start.38 = (f32[4,1,256]{2,1,0:T(1,128)S(1)}, f32[4,1,256]{2,1,0:T(1,128)}, u32[]{:S(2)}) copy-start(f32[4,1,256]{2,1,0:T(1,128)} %copy-done.37) | copy-start | bytes 12292
  552.4 154.4 %copy-start.46 = (f32[4,1,256]{2,1,0:T(1,128)S(1)}, f32[4,1,256]{2,1,0:T(1,128)}, u32[]{:S(2)}) copy-start(f32[4,1,256]{2,1,0:T(1,128)} %copy-done.45) | copy-start | bytes 12292
  725.0 421.1 %reduce-scatter.12.cloned.1.call-start = ((), (), s32[]{:S(2)}) async-start(), calls=%async_computation.12 | async-start | bytes 10485760 | tf_op jit(solution)/shard_map/reduce_scatter | solution.py:336
  746.7 546.6 %reduce-scatter.14.cloned.1.call-start = ((), (), s32[]{:S(2)}) async-start(), calls=%async_computation.13 | async-start | bytes 10485760 | tf_op jit(solution)/shard_map/reduce_scatter | solution.py:339
  766.9 92.6 %copy-start.58 = (bf16[256]{0:T(256)(128)(2,1)S(1)}, bf16[256]{0:T(256)(128)(2,1)}, u32[]{:S(2)}) copy-start(bf16[256]{0:T(256)(128)(2,1)} %param.41) | copy-start | bytes 1540
  766.9 548.9 %reduce-scatter.6.cloned.1.call-start = ((), (), s32[]{:S(2)}) async-start(), calls=%async_computation.9 | async-start | bytes 143360 | tf_op jit(solution)/shard_map/reduce_scatter | solution.py:369
  768.5 72.6 %collective-permute-start = (bf16[1024,1024]{1,0:T(8,128)(2,1)S(1)}, bf16[1024,1024]{1,0:T(8,128)(2,1)}, u32[]{:S(2)}, u32[]{:S(2)}) collective-permute-start(bf16[1024,1024]{1,0:T(8,128)(2,1)S(1)} %copy-done.11), channel_id=1, source_target_pairs={{0,1},{1,2},{2,3},{3,0},{4,5},{5,6},{6,7},{7,4},{8,9},{9,10},{10,1... | collective-permute-start | bytes 6291464 | tf_op jit(solution)/shard_map/ppermute | solution.py:25
  841.0 175.1 %collective-permute-start.1 = (bf16[1024,1024]{1,0:T(8,128)(2,1)}, bf16[1024,1024]{1,0:T(8,128)(2,1)}, u32[]{:S(2)}, u32[]{:S(2)}) collective-permute-start(bf16[1024,1024]{1,0:T(8,128)(2,1)} %collective-permute-done), channel_id=1, source_target_pairs={{0,1},{1,2},{2,3},{3,0},{4,5},{5,6},{6,7},{7,4},{8,9},{9,10},{10,1... | collective-permute-start | bytes 6291464 | tf_op jit(solution)/shard_map/ppermute | solution.py:25
  853.9 169.9 %collective-permute-start.2 = (bf16[1024,1024]{1,0:T(8,128)(2,1)S(1)}, bf16[1024,1024]{1,0:T(8,128)(2,1)}, u32[]{:S(2)}, u32[]{:S(2)}) collective-permute-start(bf16[1024,1024]{1,0:T(8,128)(2,1)S(1)} %copy-done.11), channel_id=1, source_target_pairs={{0,3},{1,0},{2,1},{3,2},{4,7},{5,4},{6,5},{7,6},{8,11},{9,8},{10,9... | collective-permute-start | bytes 6291464 | tf_op jit(solution)/shard_map/ppermute | solution.py:27
  1094.0 329.8 %all-reduce.14.cloned.1.call-start = ((), (), s32[]{:S(2)}) async-start(), calls=%async_computation.14 | async-start | bytes 12582912 | tf_op jit(solution)/shard_map/psum | solution.py:375
  (45 other events, 781.7 us)
Sparse Core Ops, SparseCore 0:
  9.7 120.2 all-gather.12
  131.5 44.0 all-gather.14
  177.2 148.3 all-gather.16
  327.1 147.8 all-gather.18
  544.0 42.0 reduce-scatter.9
  725.1 273.7 reduce-scatter.7
  1001.4 144.6 reduce-scatter.11
  1148.6 144.5 reduce-scatter.13
  1295.6 19.8 reduce-scatter.5
  1320.1 103.5 all-reduce.13
